TPU v7x, 512 devices: a whole 4x8x8 slice. The times are simulated.
512 devices in a mesh: dp: 2 (over y_hi), gx: 32 (over x, z), gy: 8 (over y_lo, core).
Axes of the slice: x: 4, y: 8 (y_hi: 2, y_lo: 4; y = y_hi * 4 + y_lo), z: 8, core: 2. Of those that a mesh axis runs over, the one named last changes fastest.
Arguments:
- fields: bfloat16 [2, 16, 256, 32768], P('dp', None, 'gx', 'gy'), may hold values from -6 to 6
- pre_act: bfloat16 [2, 16, 256, 32768], P('dp', None, 'gx', 'gy'), may hold values from -6 to 6
- cotangent: bfloat16 [2, 16, 256, 32768], P('dp', None, 'gx', 'gy'), may hold values from -6 to 6
- spec_weight: bfloat16 [2, 32, 32, 16, 256], P(None, 'gx', None, 'gy'), may hold values from -12 to 12
- point_weight: bfloat16 [16, 16], replicated, may hold values from -1.5 to 1.5
Outputs:
- grad_fields: bfloat16 [2, 16, 256, 32768], P('dp', None, 'gx', 'gy')
- grad_spec: float32 [2, 32, 32, 16, 256], P(None, 'gx', None, 'gy')
All inputs are finite; a program needn't handle non-finite values.
Results may differ from a plain program's by a relative error of at most 0.0098.
Values may be sent and summed in bfloat16 or wider, within the bound.
No kernel may reach another device: no remote copies, remote signals or barrier semaphores. Data moves between devices by JAX's collectives and lax.ppermute only.
A program may use at most 64 MiB of HBM per device.

v0:
```python
import math
import jax
import jax.numpy as jnp
from jax import lax
from jax.sharding import PartitionSpec as P

C = 16
NX = 256
NY = 512
NZ = 64
MX = 32
MY = 32
MZ = 16


def kept_freqs(kept, length, both_signs):
    index = jnp.arange(kept, dtype=jnp.int32)
    if both_signs:
        return jnp.where(index < kept // 2, index, length - kept + index)
    return index


def phase(freqs, points, length):
    turns = points[:, None] * freqs[None, :] % length
    return turns.astype(jnp.float32) * (2.0 * math.pi / length)


def forward_table(kept, length):
    angle = phase(kept_freqs(kept, length, True), jnp.arange(length, dtype=jnp.int32), length)
    cosine = jnp.cos(angle)
    minus_sine = -jnp.sin(angle)
    upper = jnp.stack([cosine, minus_sine], axis=-1)
    lower = jnp.stack([-minus_sine, cosine], axis=-1)
    return jnp.stack([upper, lower], axis=1).astype(jnp.bfloat16)


def inverse_table(kept, length, positions):
    angle = phase(kept_freqs(kept, length, True), positions, length)
    cosine = jnp.transpose(jnp.cos(angle))
    sine = jnp.transpose(jnp.sin(angle))
    upper = jnp.stack([cosine, sine], axis=-1)
    lower = jnp.stack([-sine, cosine], axis=-1)
    return jnp.stack([upper, lower], axis=1).astype(jnp.bfloat16)


def z_forward_table():
    angle = phase(kept_freqs(MZ, NZ, False), jnp.arange(NZ, dtype=jnp.int32), NZ)
    return (
        jnp.stack([jnp.cos(angle), -jnp.sin(angle)], axis=-1)
        .reshape(NZ, 2 * MZ)
        .astype(jnp.bfloat16)
    )


def z_inverse_table():
    angle = jnp.transpose(phase(kept_freqs(MZ, NZ, False), jnp.arange(NZ, dtype=jnp.int32), NZ))
    return (
        jnp.stack([jnp.cos(angle), -jnp.sin(angle)], axis=1)
        .reshape(2 * MZ, NZ)
        .astype(jnp.bfloat16)
    )


def gelu_slope(value):
    cdf = 0.5 * (1.0 + jax.scipy.special.erf(value * (1.0 / math.sqrt(2.0))))
    return cdf + value * jnp.exp(-0.5 * value * value) * (1.0 / math.sqrt(2.0 * math.pi))


def scale_modes(mode_values, weight_z):
    return mode_values.astype(jnp.float32) * weight_z[:, None]


def weight_grads(field_hat, grad_scaled):
    highest = lax.Precision.HIGHEST
    real_u = field_hat[..., 0].astype(jnp.float32)
    imag_u = field_hat[..., 1].astype(jnp.float32)
    real_d = grad_scaled[..., 0]
    imag_d = grad_scaled[..., 1]
    form = "bixyz,boxyz->xyzio"
    real_w = jnp.einsum(form, real_u, real_d, precision=highest) + jnp.einsum(
        form, imag_u, imag_d, precision=highest
    )
    imag_w = jnp.einsum(form, real_u, imag_d, precision=highest) - jnp.einsum(
        form, imag_u, real_d, precision=highest
    )
    result = jnp.stack([real_w, imag_w], axis=0)
    return result.reshape(result.shape[:4] + (C * C,))


def input_grads(spec_weight, grad_scaled):
    highest = lax.Precision.HIGHEST
    weights = spec_weight.astype(jnp.float32).reshape(spec_weight.shape[:4] + (C, C))
    real_d = grad_scaled[..., 0]
    imag_d = grad_scaled[..., 1]
    form = "xyzio,boxyz->bixyz"
    real_g = jnp.einsum(form, weights[0], real_d, precision=highest) + jnp.einsum(
        form, weights[1], imag_d, precision=highest
    )
    imag_g = jnp.einsum(form, weights[0], imag_d, precision=highest) - jnp.einsum(
        form, weights[1], real_d, precision=highest
    )
    return jnp.stack([real_g, imag_g], axis=-1).astype(jnp.bfloat16)


def on_device(fields, pre_act, cotangent, spec_weight, point_weight):
    count_x = lax.axis_size("gx")
    count_y = lax.axis_size("gy")
    local_batch, channels, local_x, local_yz = fields.shape
    local_y = local_yz // NZ
    sub_y = local_y // count_x
    local_mx = spec_weight.shape[1]
    local_mz = spec_weight.shape[3]
    stack_rows = 2 * local_batch * channels
    half_rows = local_batch * channels
    grad_pre = (cotangent.astype(jnp.float32) * gelu_slope(pre_act.astype(jnp.float32))).astype(
        jnp.bfloat16
    )
    stacked = jnp.concatenate([fields, grad_pre], axis=0)
    z_forward = z_forward_table()
    arrived = lax.all_to_all(
        stacked.reshape(stack_rows, local_x, local_yz),
        "gx",
        split_axis=2,
        concat_axis=1,
        tiled=True,
    )
    z_spectra = jnp.dot(
        arrived.reshape(stack_rows, NX, sub_y, NZ), z_forward, preferred_element_type=jnp.float32
    ).astype(jnp.bfloat16)
    z_spectra = z_spectra.reshape(stack_rows, NX, sub_y, MZ, 2)
    x_spectra = jnp.einsum(
        "sxyzr,xrkq->skyzq", z_spectra, forward_table(MX, NX), preferred_element_type=jnp.float32
    ).astype(jnp.bfloat16)
    x_spectra = x_spectra.reshape(stack_rows, MX, sub_y, 2 * MZ)
    mode_lines = lax.all_to_all(
        lax.all_to_all(x_spectra, "gx", split_axis=1, concat_axis=2, tiled=True),
        "gy",
        split_axis=3,
        concat_axis=2,
        tiled=True,
    )
    mode_lines = mode_lines.reshape(stack_rows, local_mx, NY, local_mz, 2)
    spectrum = jnp.einsum(
        "skyzr,yrlq->sklzq", mode_lines, forward_table(MY, NY), preferred_element_type=jnp.float32
    ).astype(jnp.bfloat16)
    spectrum = spectrum.reshape(2, local_batch, channels, local_mx, MY, local_mz, 2)
    field_hat = spectrum[0]
    grad_hat_in = spectrum[1]
    kz_index = lax.axis_index("gy") * local_mz + jnp.arange(local_mz, dtype=jnp.int32)
    weight_z = jnp.where(kz_index == 0, 1.0, 2.0).astype(jnp.float32) / float(NX * NY * NZ)
    grad_scaled = scale_modes(grad_hat_in, weight_z)
    grad_spec = lax.psum(weight_grads(field_hat, grad_scaled).astype(jnp.bfloat16), "dp").astype(
        jnp.float32
    )
    grad_hat = input_grads(spec_weight, grad_scaled).reshape(half_rows, local_mx, MY, local_mz, 2)
    span = count_y * sub_y
    order = jnp.arange(NY, dtype=jnp.int32)
    block = order // span
    rest = order % span
    positions = rest // sub_y * local_y + block * sub_y + rest % sub_y
    back_y = jnp.einsum(
        "sklzr,lryq->skyzq",
        grad_hat,
        inverse_table(MY, NY, positions),
        preferred_element_type=jnp.float32,
    ).astype(jnp.bfloat16)
    back_y = back_y.reshape(half_rows, local_mx, NY, 2 * local_mz)
    spread = lax.all_to_all(
        lax.all_to_all(back_y, "gx", split_axis=2, concat_axis=1, tiled=True),
        "gy",
        split_axis=2,
        concat_axis=3,
        tiled=True,
    )
    spread = spread.reshape(half_rows, MX, sub_y, MZ, 2)
    back_x = jnp.einsum(
        "skyzr,krxq->sxyzq",
        spread,
        inverse_table(MX, NX, jnp.arange(NX, dtype=jnp.int32)),
        preferred_element_type=jnp.float32,
    ).astype(jnp.bfloat16)
    returned = lax.all_to_all(
        back_x.reshape(half_rows, NX, sub_y * 2 * MZ), "gx", split_axis=1, concat_axis=2, tiled=True
    )
    spectral = jnp.dot(
        returned.reshape(half_rows, local_x, local_y, 2 * MZ),
        z_inverse_table(),
        preferred_element_type=jnp.float32,
    )
    spectral = spectral.reshape(local_batch, channels, local_x, local_yz)
    pointwise = jnp.einsum(
        "io,boxq->bixq", point_weight, grad_pre, preferred_element_type=jnp.float32
    )
    grad_fields = (spectral + pointwise).astype(jnp.bfloat16)
    return (grad_fields, grad_spec)


def solution(mesh):
    placed = (
        P("dp", None, "gx", "gy"),
        P("dp", None, "gx", "gy"),
        P("dp", None, "gx", "gy"),
        P(None, "gx", None, "gy", None),
        P(),
    )
    return jax.shard_map(
        on_device,
        mesh=mesh,
        in_specs=placed,
        out_specs=(P("dp", None, "gx", "gy"), P(None, "gx", None, "gy", None)),
        check_vma=False,
    )
```

profile of v0, /device:TPU:1, one launch (start us, length us, event | category | flops | bytes accessed | tf_op | source)
XLA Modules:
  0.0 255.6 jit_solution(6188466090925207576)
XLA Ops:
  7.2 2.3 fusion.11
  9.7 8.1 %copy.200 = bf16[32,8,4096]{0,1,2:T(8,128)(2,1)} copy(bf16[32,8,4096]{2,1,0:T(8,128)(2,1)S(1)} %bitcast.226) | data formatting | bytes 4194304 | tf_op jit(solution)/shard_map/reshape | solution.py:121
  17.8 13.3 %reshape.1022 = bf16[32,2,16384]{2,1,0:T(2,128)(2,1)} reshape(bf16[4096,8,32]{2,1,0:T(8,128)(2,1)} %bitcast.223) | data formatting | bytes 4194304
  31.1 13.8 %all-to-all-start = ((bf16[32,2,16384]{2,1,0:T(2,128)(2,1)}), bf16[32,2,16384]{2,1,0:T(2,128)(2,1)S(1)}, u32[]{:S(2)}, u32[]{:S(2)}) async-start(bf16[32,2,16384]{2,1,0:T(2,128)(2,1)} %reshape.1022), calls=%async_computation | async-start | bytes 4194304 | tf_op jit(solution)/shard_map/all_to_all | solution.py:120
  45.4 0.3 negate_convert_fusion
  45.7 48.1 %all-to-all-done = bf16[32,2,16384]{2,1,0:T(2,128)(2,1)S(1)} async-done(((bf16[32,2,16384]{2,1,0:T(2,128)(2,1)}), bf16[32,2,16384]{2,1,0:T(2,128)(2,1)S(1)}, u32[]{:S(2)}, u32[]{:S(2)}) %all-to-all-start) | async-done | bytes 2097184 | tf_op jit(solution)/shard_map/all_to_all | solution.py:120
  93.9 6.6 %reshape.1023 = bf16[4096,8,32]{2,1,0:T(8,128)(2,1)} reshape(bf16[32,2,16384]{2,1,0:T(2,128)(2,1)S(1)} %all-to-all-done) | data formatting | bytes 4194304
  100.4 9.2 %copy.202 = bf16[32,32,8,128]{3,2,1,0:T(8,128)(2,1)S(1)} copy(bf16[32,32,8,128]{0,2,3,1:T(8,128)(2,1)} %bitcast.224) | data formatting | bytes 4194304 | tf_op jit(solution)/shard_map/all_to_all | solution.py:120
  109.7 3.3 %reshape.979 = bf16[32,256,2,64]{3,2,1,0:T(2,128)(2,1)} reshape(bf16[32,32,8,128]{3,2,1,0:T(8,128)(2,1)S(1)} %copy.202) | data formatting | bytes 4194304 | tf_op jit(solution)/shard_map/reshape | solution.py:128
  113.0 3.7 %fusion.12 = bf16[32,256,2,32]{1,3,2,0:T(8,128)(2,1)S(1)} fusion(bf16[64,32,1,1]{0,1,3,2:T(8,128)(2,1)S(1)} %bitcast.246, bf16[32,256,2,64]{3,2,1,0:T(2,128)(2,1)} %reshape.979), kind=kOutput, calls=%fused_computation.18 | convolution fusion | flops 67633152 | bytes 3149824 | tf_op jit(solution)/shard_map/dot_general | solution.py:127
  116.7 0.6 copy.272
  117.3 1.0 fusion.18
  118.2 0.3 copy.206
  118.5 0.9 copy.207
  119.4 1.2 reshape.1024
  120.6 7.0 %all-to-all-start.1 = ((bf16[32,2,1024]{2,1,0:T(2,128)(2,1)}), bf16[32,2,1024]{2,1,0:T(2,128)(2,1)S(1)}, u32[]{:S(2)}, u32[]{:S(2)}) async-start(bf16[32,2,1024]{2,1,0:T(2,128)(2,1)} %reshape.1024), calls=%async_computation.1 | async-start | bytes 262144 | tf_op jit(solution)/shard_map/all_to_all | solution.py:136
  127.9 0.3 fusion.58
  128.3 8.5 %all-to-all-done.1 = bf16[32,2,1024]{2,1,0:T(2,128)(2,1)S(1)} async-done(((bf16[32,2,1024]{2,1,0:T(2,128)(2,1)}), bf16[32,2,1024]{2,1,0:T(2,128)(2,1)S(1)}, u32[]{:S(2)}, u32[]{:S(2)}) %all-to-all-start.1) | async-done | bytes 131104 | tf_op jit(solution)/shard_map/all_to_all | solution.py:136
  136.8 0.3 reshape.1025
  137.0 0.6 copy.209
  137.6 0.9 reshape.1026
  138.5 7.2 %all-to-all-start.2 = ((bf16[8,2,4096]{2,1,0:T(2,128)(2,1)}), bf16[8,2,4096]{2,1,0:T(2,128)(2,1)S(1)}, u32[]{:S(2)}, u32[]{:S(2)}) async-start(bf16[8,2,4096]{2,1,0:T(2,128)(2,1)} %reshape.1026), calls=%async_computation.2 | async-start | bytes 262144 | tf_op jit(solution)/shard_map/all_to_all | solution.py:135
  145.8 5.7 %all-to-all-done.2 = bf16[8,2,4096]{2,1,0:T(2,128)(2,1)S(1)} async-done(((bf16[8,2,4096]{2,1,0:T(2,128)(2,1)}), bf16[8,2,4096]{2,1,0:T(2,128)(2,1)S(1)}, u32[]{:S(2)}, u32[]{:S(2)}) %all-to-all-start.2) | async-done | bytes 131104 | tf_op jit(solution)/shard_map/all_to_all | solution.py:135
  152.4 0.3 fusion.24
  153.0 0.3 copy.214
  153.3 0.6 reshape.1028
  153.9 12.2 %all_to_all.84 = bf16[32,2,512]{2,1,0:T(2,128)(2,1)S(1)} all-to-all(bf16[32,2,512]{2,1,0:T(2,128)(2,1)S(1)} %reshape.1028), channel_id=1, replica_groups=mesh['dp'=2,'gx'=32,'gy'=8] {'gx'}, dimensions={0} | all-to-all | bytes 131072 | tf_op jit(solution)/shard_map/all_to_all | solution.py:169
  166.0 0.4 reshape.1029
  166.4 0.6 copy.216
  167.0 0.9 reshape.1030
  167.9 5.7 %all-to-all-start.4 = ((bf16[8,2,2048]{2,1,0:T(2,128)(2,1)}), bf16[8,2,2048]{2,1,0:T(2,128)(2,1)S(1)}, u32[]{:S(2)}, u32[]{:S(2)}) async-start(bf16[8,2,2048]{2,1,0:T(2,128)(2,1)} %reshape.1030), calls=%async_computation.4 | async-start | bytes 131072 | tf_op jit(solution)/shard_map/all_to_all | solution.py:168
  173.8 4.9 %all-to-all-done.4 = bf16[8,2,2048]{2,1,0:T(2,128)(2,1)S(1)} async-done(((bf16[8,2,2048]{2,1,0:T(2,128)(2,1)}), bf16[8,2,2048]{2,1,0:T(2,128)(2,1)S(1)}, u32[]{:S(2)}, u32[]{:S(2)}) %all-to-all-start.4) | async-done | bytes 65568 | tf_op jit(solution)/shard_map/all_to_all | solution.py:168
  178.9 0.3 fusion.17
  179.2 0.3 copy.219
  179.5 1.3 copy.220
  180.8 1.5 reshape.1032
  182.4 3.9 %all-to-all-start.5 = ((bf16[32,2,4096]{2,1,0:T(2,128)(2,1)}), bf16[32,2,4096]{2,1,0:T(2,128)(2,1)S(1)}, u32[]{:S(2)}, u32[]{:S(2)}) async-start(bf16[32,2,4096]{2,1,0:T(2,128)(2,1)} %reshape.1032), calls=%async_computation.5 | async-start | bytes 1048576 | tf_op jit(solution)/shard_map/all_to_all | solution.py:182
  186.3 0.3 all-reduce.2.cloned.1.call-start
  186.9 0.6 pad_maximum_fusion.1
  187.6 44.5 %all-reduce.2.cloned.1.call-done = bf16[2,1,32,2,256]{4,2,3,1,0:T(8,128)(2,1)} async-done(((bf16[2,1,32,2,256]{4,2,3,1,0:T(8,128)(2,1)}), bf16[2,1,32,2,256]{4,2,3,1,0:T(8,128)(2,1)}) %all-reduce.2.cloned.1.call-update) | async-done | bytes 65552 | tf_op jit(solution)/shard_map/psum | solution.py:152
  232.1 1.6 copy.230
  233.7 0.7 reshape.1033
  234.4 1.7 copy.222
  236.0 2.7 %reshape.990 = bf16[16,8,64,32]{3,2,1,0:T(8,128)(2,1)S(1)} reshape(bf16[16,8,32,64]{3,2,1,0:T(8,128)(2,1)} %copy.222) | data formatting | bytes 1048576 | tf_op jit(solution)/shard_map/reshape | solution.py:186
  238.7 2.6 %fusion.103 = f32[16,8,64,64]{3,2,1,0:T(8,128)} fusion(bf16[16,8,64,32]{3,2,1,0:T(8,128)(2,1)S(1)} %reshape.990, bf16[32,64,1,1]{1,0,3,2:T(8,128)(2,1)S(1)} %bitcast.247), kind=kOutput, calls=%fused_computation.190 | convolution fusion | flops 33554432 | bytes 2625536 | tf_op jit(solution)/shard_map/dot_general | solution.py:185
  241.4 3.5 %reshape.991 = f32[1,16,8,4096]{3,2,1,0:T(8,128)S(1)} reshape(f32[16,8,64,64]{3,2,1,0:T(8,128)} %fusion.103) | data formatting | bytes 4194304 | tf_op jit(solution)/shard_map/reshape | solution.py:190
  244.9 2.3 fusion.1
  247.2 1.6 copy.229
  (45 shorter events, 2.8 us)
Async XLA Ops:
  7.2 237.8 %copy-start = (bf16[16,16]{1,0:T(8,128)(2,1)S(1)}, bf16[16,16]{1,0:T(8,128)(2,1)}, u32[]{:S(2)}) copy-start(bf16[16,16]{1,0:T(8,128)(2,1)} %param.9) | copy-start | bytes 1540
  7.2 2.3 copy-start.1
  31.1 14.2 %copy-start.2 = (bf16[2,1,32,2,256]{4,3,2,1,0:T(2,128)(2,1)S(1)}, bf16[2,1,32,2,256]{4,3,2,1,0:T(2,128)(2,1)}, u32[]{:S(2)}) copy-start(bf16[2,1,32,2,256]{4,3,2,1,0:T(2,128)(2,1)} %param.8) | copy-start | bytes 196612
  31.1 62.7 %all-to-all-start = ((bf16[32,2,16384]{2,1,0:T(2,128)(2,1)}), bf16[32,2,16384]{2,1,0:T(2,128)(2,1)S(1)}, u32[]{:S(2)}, u32[]{:S(2)}) async-start(bf16[32,2,16384]{2,1,0:T(2,128)(2,1)} %reshape.1022), calls=%async_computation | async-start | bytes 4194304 | tf_op jit(solution)/shard_map/all_to_all | solution.py:120
  120.6 16.2 %all-to-all-start.1 = ((bf16[32,2,1024]{2,1,0:T(2,128)(2,1)}), bf16[32,2,1024]{2,1,0:T(2,128)(2,1)S(1)}, u32[]{:S(2)}, u32[]{:S(2)}) async-start(bf16[32,2,1024]{2,1,0:T(2,128)(2,1)} %reshape.1024), calls=%async_computation.1 | async-start | bytes 262144 | tf_op jit(solution)/shard_map/all_to_all | solution.py:136
  138.5 13.0 %all-to-all-start.2 = ((bf16[8,2,4096]{2,1,0:T(2,128)(2,1)}), bf16[8,2,4096]{2,1,0:T(2,128)(2,1)S(1)}, u32[]{:S(2)}, u32[]{:S(2)}) async-start(bf16[8,2,4096]{2,1,0:T(2,128)(2,1)} %reshape.1026), calls=%async_computation.2 | async-start | bytes 262144 | tf_op jit(solution)/shard_map/all_to_all | solution.py:135
  167.9 10.7 %all-to-all-start.4 = ((bf16[8,2,2048]{2,1,0:T(2,128)(2,1)}), bf16[8,2,2048]{2,1,0:T(2,128)(2,1)S(1)}, u32[]{:S(2)}, u32[]{:S(2)}) async-start(bf16[8,2,2048]{2,1,0:T(2,128)(2,1)} %reshape.1030), calls=%async_computation.4 | async-start | bytes 131072 | tf_op jit(solution)/shard_map/all_to_all | solution.py:168
  182.4 51.3 %all-to-all-start.5 = ((bf16[32,2,4096]{2,1,0:T(2,128)(2,1)}), bf16[32,2,4096]{2,1,0:T(2,128)(2,1)S(1)}, u32[]{:S(2)}, u32[]{:S(2)}) async-start(bf16[32,2,4096]{2,1,0:T(2,128)(2,1)} %reshape.1032), calls=%async_computation.5 | async-start | bytes 1048576 | tf_op jit(solution)/shard_map/all_to_all | solution.py:182
  186.3 45.8 %all-reduce.2.cloned.1.call-start = ((), (), s32[]{:S(2)}) async-start(), calls=%async_computation.6 | async-start | bytes 131072 | tf_op jit(solution)/shard_map/psum | solution.py:152
Sparse Core Ops, SparseCore 0:
  190.5 41.5 all-reduce.1
where the time goes:
time: 257 us; the launch traced here: 256 us
  waiting for transfers between devices  112 us (44%)
  local copies, waits for them, and re-layouts  64.1 us (25%)
  starting transfers between devices  37.9 us (15%)
  between operations  14.5 us (6%)
  blocking collectives  12.2 us (5%)
  matrix products  10.3 us (4%)
  other arithmetic  4.89 us (2%)
    all_to_all x1, waiting for transfers between devices, on_device(): lax.all_to_all(stacked.reshape(stack_rows, local_x, local_yz), 'gx', spli...  48.1 us
    psum x1, waiting for transfers between devices, on_device(): lax.psum(weight_grads(field_hat, grad_scaled).astype(jnp.bfloat16), 'dp')  44.5 us
    unnamed x23, local copies, waits for them, and re-layouts  30.1 us
    all_to_all x1, starting transfers between devices, on_device(): lax.all_to_all(stacked.reshape(stack_rows, local_x, local_yz), 'gx', spli...  13.8 us
    all_to_all x1, blocking collectives, on_device(): lax.all_to_all(back_y, 'gx', split_axis=2, concat_axis=1, tiled=True)  12.2 us
    all_to_all x1, local copies, waits for them, and re-layouts, on_device(): lax.all_to_all(stacked.reshape(stack_rows, local_x, local_yz), 'gx', spli...  9.24 us
    all_to_all x1, waiting for transfers between devices, on_device(): lax.all_to_all(x_spectra, 'gx', split_axis=1, concat_axis=2, tiled=True)  8.52 us
    reshape x1, local copies, waits for them, and re-layouts, on_device(): stacked.reshape(stack_rows, local_x, local_yz)  8.08 us
  transfers between devices with their start and end apart: 6, of which 5 were waited for; matrix products, arithmetic and copies ran while one was open for 2% of the time, Pallas kernels for 0%

commit v1 on v0

--- a/solution.py
+++ b/solution.py
@@ -149,9 +149,9 @@
     kz_index = lax.axis_index("gy") * local_mz + jnp.arange(local_mz, dtype=jnp.int32)
     weight_z = jnp.where(kz_index == 0, 1.0, 2.0).astype(jnp.float32) / float(NX * NY * NZ)
     grad_scaled = scale_modes(grad_hat_in, weight_z)
-    grad_spec = lax.psum(weight_grads(field_hat, grad_scaled).astype(jnp.bfloat16), "dp").astype(
-        jnp.float32
-    )
+    grad_spec = jnp.sum(
+        lax.all_gather(weight_grads(field_hat, grad_scaled).astype(jnp.bfloat16), "dp"), axis=0
+    ).astype(jnp.float32)
     grad_hat = input_grads(spec_weight, grad_scaled).reshape(half_rows, local_mx, MY, local_mz, 2)
     span = count_y * sub_y
     order = jnp.arange(NY, dtype=jnp.int32)

time: 257 us -> 213 us (0.83)
  waiting for transfers between devices: 112 us -> 80.9 us
  between operations: 14.5 us -> 1.08 us
  blocking collectives: 12.2 us -> 8.01 us
  starting transfers between devices: 37.9 us -> 41.2 us
    psum x1 -> x0, waiting for transfers between devices: 44.5 us -> none  [on_device(): lax.psum(weight_grads(field_hat, grad_scaled).astype(jnp.bfloat16), 'dp')]
    all_to_all x1 -> x0, blocking collectives: 12.2 us -> none  [on_device(): lax.all_to_all(back_y, 'gx', split_axis=2, concat_axis=1, tiled=True)]
    all_to_all x0 -> x1, waiting for transfers between devices: none -> 8.58 us  [on_device(): lax.all_to_all(back_y, 'gx', split_axis=2, concat_axis=1, tiled=True)]
    all_gather x0 -> x1, blocking collectives: none -> 8.01 us  [on_device(): lax.all_gather(weight_grads(field_hat, grad_scaled).astype(jnp.bfloat16),...]
    all_to_all x1, waiting for transfers between devices: 0.01 us -> 4.85 us  [on_device(): lax.all_to_all(back_x.reshape(half_rows, NX, sub_y * 2 * MZ), 'gx', split...]
    all_to_all x0 -> x1, starting transfers between devices: none -> 3.85 us  [on_device(): lax.all_to_all(back_y, 'gx', split_axis=2, concat_axis=1, tiled=True)]
    unnamed x23 -> x24, local copies, waits for them, and re-layouts: 30.1 us -> 30.1 us
  transfers between devices with their start and end apart: 6 -> 6, of which waited for: 5 -> 6; matrix products, arithmetic and copies ran while one was open for 2% -> 1% of each run, Pallas kernels for 0% -> 0%
where the time goes in v1:
time: 213 us; the launch traced here: 210 us
  waiting for transfers between devices  80.9 us (38%)
  local copies, waits for them, and re-layouts  64.1 us (30%)
  starting transfers between devices  41.2 us (19%)
  matrix products  10.3 us (5%)
  blocking collectives  8.01 us (4%)
  other arithmetic  4.31 us (2%)
    all_to_all x1, waiting for transfers between devices, on_device(): lax.all_to_all(stacked.reshape(stack_rows, local_x, local_yz), 'gx', spli...  48.1 us
    unnamed x24, local copies, waits for them, and re-layouts  30.1 us
    all_to_all x1, starting transfers between devices, on_device(): lax.all_to_all(stacked.reshape(stack_rows, local_x, local_yz), 'gx', spli...  13.8 us
    all_to_all x1, local copies, waits for them, and re-layouts, on_device(): lax.all_to_all(stacked.reshape(stack_rows, local_x, local_yz), 'gx', spli...  9.24 us
    all_to_all x1, waiting for transfers between devices, on_device(): lax.all_to_all(back_y, 'gx', split_axis=2, concat_axis=1, tiled=True)  8.58 us
    all_to_all x1, waiting for transfers between devices, on_device(): lax.all_to_all(x_spectra, 'gx', split_axis=1, concat_axis=2, tiled=True)  8.52 us
    reshape x1, local copies, waits for them, and re-layouts, on_device(): stacked.reshape(stack_rows, local_x, local_yz)  8.04 us
    all_gather x1, blocking collectives, on_device(): lax.all_gather(weight_grads(field_hat, grad_scaled).astype(jnp.bfloat16),...  8.01 us
  transfers between devices with their start and end apart: 6, of which 6 were waited for; matrix products, arithmetic and copies ran while one was open for 1% of the time, Pallas kernels for 0%

profile of v1, /device:TPU:1, one launch (start us, length us, event | category | flops | bytes accessed | tf_op | source)
XLA Modules:
  0.0 209.9 jit_solution(12966531480754730534)
XLA Ops:
  0.7 2.3 %fusion.11 = bf16[1,16,8,4096]{3,2,1,0:T(8,128)(2,1)S(1)} fusion(bf16[1,16,8,4096]{3,2,1,0:T(8,128)(2,1)} %param.6, bf16[1,16,8,4096]{3,2,1,0:T(8,128)(2,1)} %param.7), kind=kLoop, calls=%fused_computation.17 | loop fusion | flops 6291456 | bytes 3145728 | tf_op jit(solution)/shard_map/convert_element_type | solution.py:115
  3.2 8.0 %copy.202 = bf16[32,8,4096]{0,1,2:T(8,128)(2,1)} copy(bf16[32,8,4096]{2,1,0:T(8,128)(2,1)S(1)} %bitcast.229) | data formatting | bytes 4194304 | tf_op jit(solution)/shard_map/reshape | solution.py:121
  11.2 13.3 %reshape.1038 = bf16[32,2,16384]{2,1,0:T(2,128)(2,1)} reshape(bf16[4096,8,32]{2,1,0:T(8,128)(2,1)} %bitcast.226) | data formatting | bytes 4194304
  24.5 13.8 %all-to-all-start = ((bf16[32,2,16384]{2,1,0:T(2,128)(2,1)}), bf16[32,2,16384]{2,1,0:T(2,128)(2,1)S(1)}, u32[]{:S(2)}, u32[]{:S(2)}) async-start(bf16[32,2,16384]{2,1,0:T(2,128)(2,1)} %reshape.1038), calls=%async_computation | async-start | bytes 4194304 | tf_op jit(solution)/shard_map/all_to_all | solution.py:120
  38.8 0.3 negate_convert_fusion
  39.2 48.1 %all-to-all-done = bf16[32,2,16384]{2,1,0:T(2,128)(2,1)S(1)} async-done(((bf16[32,2,16384]{2,1,0:T(2,128)(2,1)}), bf16[32,2,16384]{2,1,0:T(2,128)(2,1)S(1)}, u32[]{:S(2)}, u32[]{:S(2)}) %all-to-all-start) | async-done | bytes 2097184 | tf_op jit(solution)/shard_map/all_to_all | solution.py:120
  87.3 6.5 %reshape.1039 = bf16[4096,8,32]{2,1,0:T(8,128)(2,1)} reshape(bf16[32,2,16384]{2,1,0:T(2,128)(2,1)S(1)} %all-to-all-done) | data formatting | bytes 4194304
  93.8 9.2 %copy.204 = bf16[32,32,8,128]{3,2,1,0:T(8,128)(2,1)S(1)} copy(bf16[32,32,8,128]{0,2,3,1:T(8,128)(2,1)} %bitcast.227) | data formatting | bytes 4194304 | tf_op jit(solution)/shard_map/all_to_all | solution.py:120
  103.1 3.3 %reshape.994 = bf16[32,256,2,64]{3,2,1,0:T(2,128)(2,1)} reshape(bf16[32,32,8,128]{3,2,1,0:T(8,128)(2,1)S(1)} %copy.204) | data formatting | bytes 4194304 | tf_op jit(solution)/shard_map/reshape | solution.py:128
  106.4 3.7 %fusion.12 = bf16[32,256,2,32]{1,3,2,0:T(8,128)(2,1)S(1)} fusion(bf16[64,32,1,1]{0,1,3,2:T(8,128)(2,1)S(1)} %bitcast.250, bf16[32,256,2,64]{3,2,1,0:T(2,128)(2,1)} %reshape.994), kind=kOutput, calls=%fused_computation.18 | convolution fusion | flops 67633152 | bytes 3149824 | tf_op jit(solution)/shard_map/dot_general | solution.py:127
  110.0 0.6 copy.275
  110.6 1.0 fusion.18
  111.6 0.3 copy.208
  111.9 0.9 copy.209
  112.8 1.2 reshape.1040
  113.9 7.0 %all-to-all-start.1 = ((bf16[32,2,1024]{2,1,0:T(2,128)(2,1)}), bf16[32,2,1024]{2,1,0:T(2,128)(2,1)S(1)}, u32[]{:S(2)}, u32[]{:S(2)}) async-start(bf16[32,2,1024]{2,1,0:T(2,128)(2,1)} %reshape.1040), calls=%async_computation.1 | async-start | bytes 262144 | tf_op jit(solution)/shard_map/all_to_all | solution.py:136
  121.3 0.3 fusion.58
  121.6 8.5 %all-to-all-done.1 = bf16[32,2,1024]{2,1,0:T(2,128)(2,1)S(1)} async-done(((bf16[32,2,1024]{2,1,0:T(2,128)(2,1)}), bf16[32,2,1024]{2,1,0:T(2,128)(2,1)S(1)}, u32[]{:S(2)}, u32[]{:S(2)}) %all-to-all-start.1) | async-done | bytes 131104 | tf_op jit(solution)/shard_map/all_to_all | solution.py:136
  130.1 0.3 reshape.1041
  130.4 0.6 copy.211
  131.0 0.9 reshape.1042
  131.9 7.2 %all-to-all-start.2 = ((bf16[8,2,4096]{2,1,0:T(2,128)(2,1)}), bf16[8,2,4096]{2,1,0:T(2,128)(2,1)S(1)}, u32[]{:S(2)}, u32[]{:S(2)}) async-start(bf16[8,2,4096]{2,1,0:T(2,128)(2,1)} %reshape.1042), calls=%async_computation.2 | async-start | bytes 262144 | tf_op jit(solution)/shard_map/all_to_all | solution.py:135
  139.1 5.7 %all-to-all-done.2 = bf16[8,2,4096]{2,1,0:T(2,128)(2,1)S(1)} async-done(((bf16[8,2,4096]{2,1,0:T(2,128)(2,1)}), bf16[8,2,4096]{2,1,0:T(2,128)(2,1)S(1)}, u32[]{:S(2)}, u32[]{:S(2)}) %all-to-all-start.2) | async-done | bytes 131104 | tf_op jit(solution)/shard_map/all_to_all | solution.py:135
  145.8 0.3 fusion.24
  146.3 0.3 copy.216
  146.6 1.2 reshape.1044
  147.9 3.9 %all-to-all-start.3 = ((bf16[32,2,512]{2,1,0:T(2,128)(2,1)}), bf16[32,2,512]{2,1,0:T(2,128)(2,1)S(1)}, u32[]{:S(2)}, u32[]{:S(2)}) async-start(bf16[32,2,512]{2,1,0:T(2,128)(2,1)} %reshape.1044), calls=%async_computation.3 | async-start | bytes 131072 | tf_op jit(solution)/shard_map/all_to_all | solution.py:169
  152.0 8.6 %all-to-all-done.3 = bf16[32,2,512]{2,1,0:T(2,128)(2,1)S(1)} async-done(((bf16[32,2,512]{2,1,0:T(2,128)(2,1)}), bf16[32,2,512]{2,1,0:T(2,128)(2,1)S(1)}, u32[]{:S(2)}, u32[]{:S(2)}) %all-to-all-start.3) | async-done | bytes 65568 | tf_op jit(solution)/shard_map/all_to_all | solution.py:169
  160.6 0.4 reshape.1045
  161.0 0.6 copy.218
  161.6 0.9 reshape.1046
  162.5 5.4 %all-to-all-start.4 = ((bf16[8,2,2048]{2,1,0:T(2,128)(2,1)}), bf16[8,2,2048]{2,1,0:T(2,128)(2,1)S(1)}, u32[]{:S(2)}, u32[]{:S(2)}) async-start(bf16[8,2,2048]{2,1,0:T(2,128)(2,1)} %reshape.1046), calls=%async_computation.4 | async-start | bytes 131072 | tf_op jit(solution)/shard_map/all_to_all | solution.py:168
  167.9 5.0 %all-to-all-done.4 = bf16[8,2,2048]{2,1,0:T(2,128)(2,1)S(1)} async-done(((bf16[8,2,2048]{2,1,0:T(2,128)(2,1)}), bf16[8,2,2048]{2,1,0:T(2,128)(2,1)S(1)}, u32[]{:S(2)}, u32[]{:S(2)}) %all-to-all-start.4) | async-done | bytes 65568 | tf_op jit(solution)/shard_map/all_to_all | solution.py:168
  173.2 0.3 fusion.17
  173.5 0.3 copy.221
  173.8 1.3 copy.222
  175.1 1.5 reshape.1048
  176.7 3.9 %all-to-all-start.5 = ((bf16[32,2,4096]{2,1,0:T(2,128)(2,1)}), bf16[32,2,4096]{2,1,0:T(2,128)(2,1)S(1)}, u32[]{:S(2)}, u32[]{:S(2)}) async-start(bf16[32,2,4096]{2,1,0:T(2,128)(2,1)} %reshape.1048), calls=%async_computation.5 | async-start | bytes 1048576 | tf_op jit(solution)/shard_map/all_to_all | solution.py:182
  180.9 8.0 %all_gather.4 = bf16[2,2,1,32,2,256]{5,3,4,2,1,0:T(8,128)(2,1)S(1)} all-gather(bf16[1,2,1,32,2,256]{5,3,4,2,1,0:T(8,128)(2,1)S(1)} %pad_maximum_fusion.1), channel_id=1, replica_groups=mesh['dp'=2,'gx'=32,'gy'=8] {'dp'}, dimensions={0}, use_global_device_ids=true | all-gather | bytes 196608 | tf_op jit(solution)/shard_map/all_gather | solution.py:153
  189.1 0.8 copy.233
  190.0 4.9 %all-to-all-done.5 = bf16[32,2,4096]{2,1,0:T(2,128)(2,1)S(1)} async-done(((bf16[32,2,4096]{2,1,0:T(2,128)(2,1)}), bf16[32,2,4096]{2,1,0:T(2,128)(2,1)S(1)}, u32[]{:S(2)}, u32[]{:S(2)}) %all-to-all-start.5) | async-done | bytes 524320 | tf_op jit(solution)/shard_map/all_to_all | solution.py:182
  194.8 0.7 reshape.1049
  195.5 1.7 copy.224
  197.1 2.7 %reshape.1005 = bf16[16,8,64,32]{3,2,1,0:T(8,128)(2,1)S(1)} reshape(bf16[16,8,32,64]{3,2,1,0:T(8,128)(2,1)} %copy.224) | data formatting | bytes 1048576 | tf_op jit(solution)/shard_map/reshape | solution.py:186
  199.9 2.6 %fusion.103 = f32[16,8,64,64]{3,2,1,0:T(8,128)} fusion(bf16[16,8,64,32]{3,2,1,0:T(8,128)(2,1)S(1)} %reshape.1005, bf16[32,64,1,1]{1,0,3,2:T(8,128)(2,1)S(1)} %bitcast.249), kind=kOutput, calls=%fused_computation.191 | convolution fusion | flops 33554432 | bytes 2625536 | tf_op jit(solution)/shard_map/dot_general | solution.py:185
  202.5 3.5 %reshape.1006 = f32[1,16,8,4096]{3,2,1,0:T(8,128)S(1)} reshape(f32[16,8,64,64]{3,2,1,0:T(8,128)} %fusion.103) | data formatting | bytes 4194304 | tf_op jit(solution)/shard_map/reshape | solution.py:190
  206.1 2.3 %fusion.1 = bf16[1,16,8,4096]{3,1,2,0:T(8,128)(2,1)S(1)} fusion(f32[1,16,8,4096]{3,2,1,0:T(8,128)S(1)} %reshape.1006, bf16[16,8,4096]{2,1,0:T(8,128)(2,1)S(1)} %bitcast.228, bf16[16,16]{1,0:T(8,128)(2,1)S(1)} %copy-done), kind=kOutput, calls=%fused_computation.2 | convolution fusion | flops 17825792 | bytes 4194816 | tf_op jit(solution)/shard_map/io,boxq->bixq/dot_general | solution.py:191
  208.3 1.6 copy.232
  (47 shorter events, 3.0 us)
Async XLA Ops:
  0.6 205.4 %copy-start = (bf16[16,16]{1,0:T(8,128)(2,1)S(1)}, bf16[16,16]{1,0:T(8,128)(2,1)}, u32[]{:S(2)}) copy-start(bf16[16,16]{1,0:T(8,128)(2,1)} %param.9) | copy-start | bytes 1540
  0.6 2.3 %copy-start.1 = (bf16[1,16,8,4096]{3,2,1,0:T(8,128)(2,1)S(1)}, bf16[1,16,8,4096]{3,2,1,0:T(8,128)(2,1)}, u32[]{:S(2)}) copy-start(bf16[1,16,8,4096]{3,2,1,0:T(8,128)(2,1)} %param.5) | copy-start | bytes 3145732
  24.5 14.2 %copy-start.2 = (bf16[2,1,32,2,256]{4,3,2,1,0:T(2,128)(2,1)S(1)}, bf16[2,1,32,2,256]{4,3,2,1,0:T(2,128)(2,1)}, u32[]{:S(2)}) copy-start(bf16[2,1,32,2,256]{4,3,2,1,0:T(2,128)(2,1)} %param.8) | copy-start | bytes 196612
  24.5 62.7 %all-to-all-start = ((bf16[32,2,16384]{2,1,0:T(2,128)(2,1)}), bf16[32,2,16384]{2,1,0:T(2,128)(2,1)S(1)}, u32[]{:S(2)}, u32[]{:S(2)}) async-start(bf16[32,2,16384]{2,1,0:T(2,128)(2,1)} %reshape.1038), calls=%async_computation | async-start | bytes 4194304 | tf_op jit(solution)/shard_map/all_to_all | solution.py:120
  113.9 16.2 %all-to-all-start.1 = ((bf16[32,2,1024]{2,1,0:T(2,128)(2,1)}), bf16[32,2,1024]{2,1,0:T(2,128)(2,1)S(1)}, u32[]{:S(2)}, u32[]{:S(2)}) async-start(bf16[32,2,1024]{2,1,0:T(2,128)(2,1)} %reshape.1040), calls=%async_computation.1 | async-start | bytes 262144 | tf_op jit(solution)/shard_map/all_to_all | solution.py:136
  131.9 13.0 %all-to-all-start.2 = ((bf16[8,2,4096]{2,1,0:T(2,128)(2,1)}), bf16[8,2,4096]{2,1,0:T(2,128)(2,1)S(1)}, u32[]{:S(2)}, u32[]{:S(2)}) async-start(bf16[8,2,4096]{2,1,0:T(2,128)(2,1)} %reshape.1042), calls=%async_computation.2 | async-start | bytes 262144 | tf_op jit(solution)/shard_map/all_to_all | solution.py:135
  147.9 12.7 %all-to-all-start.3 = ((bf16[32,2,512]{2,1,0:T(2,128)(2,1)}), bf16[32,2,512]{2,1,0:T(2,128)(2,1)S(1)}, u32[]{:S(2)}, u32[]{:S(2)}) async-start(bf16[32,2,512]{2,1,0:T(2,128)(2,1)} %reshape.1044), calls=%async_computation.3 | async-start | bytes 131072 | tf_op jit(solution)/shard_map/all_to_all | solution.py:169
  162.5 10.5 %all-to-all-start.4 = ((bf16[8,2,2048]{2,1,0:T(2,128)(2,1)}), bf16[8,2,2048]{2,1,0:T(2,128)(2,1)S(1)}, u32[]{:S(2)}, u32[]{:S(2)}) async-start(bf16[8,2,2048]{2,1,0:T(2,128)(2,1)} %reshape.1046), calls=%async_computation.4 | async-start | bytes 131072 | tf_op jit(solution)/shard_map/all_to_all | solution.py:168
  176.7 18.2 %all-to-all-start.5 = ((bf16[32,2,4096]{2,1,0:T(2,128)(2,1)}), bf16[32,2,4096]{2,1,0:T(2,128)(2,1)S(1)}, u32[]{:S(2)}, u32[]{:S(2)}) async-start(bf16[32,2,4096]{2,1,0:T(2,128)(2,1)} %reshape.1048), calls=%async_computation.5 | async-start | bytes 1048576 | tf_op jit(solution)/shard_map/all_to_all | solution.py:182
